TPU v7x, 32 devices: a whole 2x2x4 slice. The times are simulated.
32 devices in a mesh: dp: 8 (over z, y), seq: 4 (over x, core).
Axes of the slice: x: 2, y: 2, z: 4, core: 2. Of those that a mesh axis runs over, the one named last changes fastest.
Arguments:
- tokens: bfloat16 [8192, 768], P(('dp', 'seq')), may hold values from -6 to 6
- ln1_gain: bfloat16 [768], P('dp'), may hold values from 0.25 to 1.75
- w_qkv: bfloat16 [768, 2304], P('dp'), may hold values from -0.21875 to 0.21875
- w_out: bfloat16 [768, 768], P('dp'), may hold values from -1.75 to 1.75
- w_ada: bfloat16 [768, 2304], P('dp'), may hold values from -0.21875 to 0.21875
- w_up: bfloat16 [768, 3072], P('dp'), may hold values from -0.21875 to 0.21875
- w_down: bfloat16 [3072, 768], P('dp'), may hold values from -0.109375 to 0.109375
- out_grad: bfloat16 [8192, 768], P(('dp', 'seq')), may hold values from -6 to 6
- layout: int32 [8, 2], P('dp'), may hold values from 256 to 896, as said below
- timestep: int32 [8], P('dp'), may hold values from 0 to 999
Outputs:
- layer_out: bfloat16 [8192, 768], P(('dp', 'seq'))
- input_grad: bfloat16 [8192, 768], P(('dp', 'seq'))
- gain_grad: float32 [768], P('dp')
- qkv_weight_grad: float32 [768, 2304], P('dp')
- out_weight_grad: float32 [768, 768], P('dp')
- ada_weight_grad: float32 [768, 2304], P('dp')
- up_weight_grad: float32 [768, 3072], P('dp')
- down_weight_grad: float32 [3072, 768], P('dp')
Inputs may be any that keep to these rules, and one draw needn't show every extreme that they name: layout[g] = (P, C): tokens below P are the prompt, the first continuation runs from P to C - 1, the second from C to 1023; P lies between 256 and 512, and each continuation holds at least a quarter of the tokens after the prompt.
All inputs are finite; a program needn't handle non-finite values.
Results may differ from a plain program's by a relative error of at most 0.017.
Values may be sent and summed in bfloat16 or wider, within the bound.
No kernel may reach another device: no remote copies, remote signals or barrier semaphores. Data moves between devices by JAX's collectives and lax.ppermute only.
A program may use at most 128 MiB of HBM per device.

v0:
```python
import math
import jax
import jax.numpy as jnp
from jax import lax
from jax.sharding import PartitionSpec as P

HEADS = 12
HEAD_DIM = 64
eps = 1e-05
neg_fill = -1e30


def layer_norm(values_in):
    average = jnp.mean(values_in, axis=-1, keepdims=True)
    centred = values_in - average
    variance = jnp.mean(centred * centred, axis=-1, keepdims=True)
    scaling = lax.rsqrt(variance + eps)
    return (centred * scaling, scaling)


def norm_back(grad_normed, normed, scaling):
    first_mean = jnp.mean(grad_normed, axis=-1, keepdims=True)
    second_mean = jnp.mean(grad_normed * normed, axis=-1, keepdims=True)
    return scaling * (grad_normed - first_mean - normed * second_mean)


def rope_tables(positions):
    half_dim = HEAD_DIM // 2
    frequency = jnp.exp(
        -math.log(10000.0) * 2.0 * jnp.arange(half_dim, dtype=jnp.float32) / HEAD_DIM
    )
    angles = positions.astype(jnp.float32)[:, None] * frequency[None, :]
    return (jnp.cos(angles), jnp.sin(angles))


def rotate(values_in, cos_table, sine_table, direction):
    half_dim = HEAD_DIM // 2
    front_half = values_in[..., :half_dim]
    back_half = values_in[..., half_dim:]
    cos_part = cos_table[:, None, :]
    sine_part = sine_table[:, None, :] * direction
    return jnp.concatenate(
        [
            front_half * cos_part - back_half * sine_part,
            back_half * cos_part + front_half * sine_part,
        ],
        axis=-1,
    )


def visible(query_pos, key_pos, prompt_end, second_start):
    query_segment = (query_pos >= prompt_end).astype(jnp.int32) + (
        query_pos >= second_start
    ).astype(jnp.int32)
    key_segment = (key_pos >= prompt_end).astype(jnp.int32) + (key_pos >= second_start).astype(
        jnp.int32
    )
    return (key_pos[None, :] < prompt_end) | (query_segment[:, None] == key_segment[None, :])


def time_table(time_steps, model_width):
    half_dim = model_width // 2
    frequency = jnp.exp(-math.log(10000.0) * jnp.arange(half_dim, dtype=jnp.float32) / half_dim)
    angles = time_steps[:, None] * frequency[None, :]
    return jnp.concatenate([jnp.cos(angles), jnp.sin(angles)], axis=1)


def left_product(left, right):
    return lax.dot_general(
        left, right, (((0,), (0,)), ((), ())), preferred_element_type=jnp.float32
    )


def right_product(left, right):
    return lax.dot_general(
        left, right, (((1,), (1,)), ((), ())), preferred_element_type=jnp.float32
    )


def split_rows(grad_full, data_count):
    return grad_full.reshape(data_count, grad_full.shape[0] // data_count, -1)


def body(tokens, ln1_gain, w_qkv, w_out, w_ada, w_up, w_down, out_grad, layout, timestep):
    seq_count = lax.axis_size("seq")
    seq_rank = lax.axis_index("seq")
    tok_rows = tokens.shape[0]
    model_width = tokens.shape[1]
    group_rows = tok_rows * seq_count
    heads_local = HEADS // seq_count
    local_width = heads_local * HEAD_DIM
    block_rows = min(512, group_rows)
    blocks = group_rows // block_rows
    gain_full, qkv_weight, out_weight = (
        lax.all_gather(ln1_gain, "dp", axis=0, tiled=True),
        lax.all_gather(w_qkv, "dp", axis=0, tiled=True),
        lax.all_gather(w_out, "dp", axis=0, tiled=True),
    )
    ada_weight, up_weight, down_weight = (
        lax.all_gather(w_ada, "dp", axis=0, tiled=True),
        lax.all_gather(w_up, "dp", axis=0, tiled=True),
        lax.all_gather(w_down, "dp", axis=0, tiled=True),
    )
    gain_float = gain_full.astype(jnp.float32)
    inputs = tokens.astype(jnp.float32)
    normed_one, scaling_one = layer_norm(inputs)
    hidden_one = (normed_one * gain_float).astype(jnp.bfloat16)
    projected = jnp.dot(hidden_one, qkv_weight, preferred_element_type=jnp.float32).reshape(
        tok_rows, 3, HEADS, HEAD_DIM
    )
    positions = seq_rank * tok_rows + jnp.arange(tok_rows, dtype=jnp.int32)
    cos_table, sine_table = rope_tables(positions)
    rotated = jnp.stack(
        [
            rotate(projected[:, 0], cos_table, sine_table, 1.0),
            rotate(projected[:, 1], cos_table, sine_table, 1.0),
            projected[:, 2],
        ],
        axis=1,
    )
    outgoing = rotated.astype(jnp.bfloat16).reshape(tok_rows, 3, seq_count, local_width)
    incoming = lax.all_to_all(outgoing, "seq", split_axis=2, concat_axis=0, tiled=True).reshape(
        group_rows, 3, heads_local, HEAD_DIM
    )
    queries = incoming[:, 0]
    keys_all = incoming[:, 1]
    values_all = incoming[:, 2]
    prompt_end = layout[0, 0]
    second_start = layout[0, 1]
    key_pos = jnp.arange(group_rows, dtype=jnp.int32)

    def scores_of(query_block, start):
        raw_scores = (
            jnp.einsum("qhd,khd->hqk", query_block, keys_all, preferred_element_type=jnp.float32)
            * 0.125
        )
        query_pos = start + jnp.arange(block_rows, dtype=jnp.int32)
        allowed = visible(query_pos, key_pos, prompt_end, second_start)
        return jnp.where(allowed[None], raw_scores, neg_fill)

    query_blocks = queries.reshape(blocks, block_rows, heads_local, HEAD_DIM)
    starts = jnp.arange(blocks, dtype=jnp.int32) * block_rows

    def forward_block(operands):
        query_block, start = operands
        scores = scores_of(query_block, start)
        row_max = jnp.max(scores, axis=-1, keepdims=True)
        exponent = jnp.exp(scores - row_max)
        row_sum = jnp.sum(exponent, axis=-1, keepdims=True)
        attn_probs = (exponent / row_sum).astype(jnp.bfloat16)
        block_out = jnp.einsum(
            "hqk,khd->qhd", attn_probs, values_all, preferred_element_type=jnp.float32
        )
        return (block_out.astype(jnp.bfloat16), (row_max + jnp.log(row_sum))[..., 0])

    attended_heads, log_sums = lax.map(forward_block, (query_blocks, starts))
    attended = lax.all_to_all(
        attended_heads.reshape(group_rows, local_width),
        "seq",
        split_axis=0,
        concat_axis=1,
        tiled=True,
    )
    middle = inputs + jnp.dot(attended, out_weight, preferred_element_type=jnp.float32)
    time_embed = time_table(timestep.astype(jnp.float32), model_width).astype(jnp.bfloat16)
    modulation = jnp.dot(time_embed, ada_weight, preferred_element_type=jnp.float32)[0]
    mod_scale = modulation[:model_width]
    mod_shift = modulation[model_width : 2 * model_width]
    mod_gate = modulation[2 * model_width :]
    normed_two, scaling_two = layer_norm(middle)
    hidden_two = (normed_two * (1.0 + mod_scale) + mod_shift).astype(jnp.bfloat16)
    pre_act = jnp.dot(hidden_two, up_weight, preferred_element_type=jnp.float32)
    gelu_vals, gelu_pull = jax.vjp(lambda inner: jax.nn.gelu(inner, approximate=True), pre_act)
    activated = gelu_vals.astype(jnp.bfloat16)
    mlp_out = jnp.dot(activated, down_weight, preferred_element_type=jnp.float32)
    result = middle + mod_gate * mlp_out
    grad_out = out_grad.astype(jnp.float32)
    grad_mlp = (mod_gate * grad_out).astype(jnp.bfloat16)
    grad_gate = jnp.sum(grad_out * mlp_out, axis=0)
    grad_wdown = left_product(activated, grad_mlp)
    grad_act = right_product(grad_mlp, down_weight)
    grad_pre = gelu_pull(grad_act)[0].astype(jnp.bfloat16)
    grad_wup = left_product(hidden_two, grad_pre)
    grad_hidden_two = right_product(grad_pre, up_weight)
    grad_scale = jnp.sum(grad_hidden_two * normed_two, axis=0)
    grad_shift = jnp.sum(grad_hidden_two, axis=0)
    grad_middle = grad_out + norm_back(grad_hidden_two * (1.0 + mod_scale), normed_two, scaling_two)
    grad_mod = jnp.concatenate([grad_scale, grad_shift, grad_gate])
    grad_branch = grad_middle.astype(jnp.bfloat16)
    grad_wout = left_product(attended, grad_branch)
    grad_attn = right_product(grad_branch, out_weight).astype(jnp.bfloat16)
    grad_heads = lax.all_to_all(grad_attn, "seq", split_axis=1, concat_axis=0, tiled=True).reshape(
        blocks, block_rows, heads_local, HEAD_DIM
    )

    def backward_block(carry, operands):
        key_grad, value_grad = carry
        query_block, start, grad_block, lse_block = operands
        scores = scores_of(query_block, start)
        attn_probs = jnp.exp(scores - lse_block[..., None])
        value_grad = value_grad + jnp.einsum(
            "hqk,qhd->khd",
            attn_probs.astype(jnp.bfloat16),
            grad_block,
            preferred_element_type=jnp.float32,
        )
        prob_grad = jnp.einsum(
            "qhd,khd->hqk", grad_block, values_all, preferred_element_type=jnp.float32
        )
        row_centre = jnp.sum(attn_probs * prob_grad, axis=-1, keepdims=True)
        score_grad = (attn_probs * (prob_grad - row_centre)).astype(jnp.bfloat16)
        query_grad = (
            jnp.einsum("hqk,khd->qhd", score_grad, keys_all, preferred_element_type=jnp.float32)
            * 0.125
        )
        key_grad = (
            key_grad
            + jnp.einsum(
                "hqk,qhd->khd", score_grad, query_block, preferred_element_type=jnp.float32
            )
            * 0.125
        )
        return ((key_grad, value_grad), query_grad)

    zero_grad = jnp.zeros((group_rows, heads_local, HEAD_DIM), jnp.float32)
    (key_grad, value_grad), query_grads = lax.scan(
        backward_block, (zero_grad, zero_grad), (query_blocks, starts, grad_heads, log_sums)
    )
    stacked = jnp.stack(
        [query_grads.reshape(group_rows, heads_local, HEAD_DIM), key_grad, value_grad], axis=1
    )
    stacked = stacked.astype(jnp.bfloat16).reshape(group_rows, 3, 1, local_width)
    returned = (
        lax.all_to_all(stacked, "seq", split_axis=0, concat_axis=2, tiled=True)
        .astype(jnp.float32)
        .reshape(tok_rows, 3, HEADS, HEAD_DIM)
    )
    grad_qkv = jnp.stack(
        [
            rotate(returned[:, 0], cos_table, sine_table, -1.0),
            rotate(returned[:, 1], cos_table, sine_table, -1.0),
            returned[:, 2],
        ],
        axis=1,
    )
    grad_qkv = grad_qkv.reshape(tok_rows, 3 * model_width).astype(jnp.bfloat16)
    grad_wqkv = left_product(hidden_one, grad_qkv)
    grad_hidden_one = right_product(grad_qkv, qkv_weight)
    grad_gain = jnp.sum(grad_hidden_one * normed_one, axis=0)
    grad_inputs = grad_middle + norm_back(grad_hidden_one * gain_float, normed_one, scaling_one)
    qkv_cols = 3 * model_width
    grad_wada = time_embed.astype(jnp.float32).reshape(-1)[:, None] * grad_mod[None, :]
    grad_joint = jnp.concatenate([grad_wqkv, grad_wada], axis=1)
    data_count = lax.axis_size("dp")
    parts = (
        lax.psum_scatter(
            split_rows(grad_gain, data_count).astype(jnp.bfloat16),
            "seq",
            scatter_dimension=1,
            tiled=True,
        ).astype(jnp.float32),
        lax.psum_scatter(
            split_rows(grad_joint, data_count).astype(jnp.bfloat16),
            "seq",
            scatter_dimension=1,
            tiled=True,
        ).astype(jnp.float32),
        lax.psum_scatter(
            split_rows(grad_wout, data_count).astype(jnp.bfloat16),
            "seq",
            scatter_dimension=1,
            tiled=True,
        ).astype(jnp.float32),
        lax.psum_scatter(
            split_rows(grad_wup, data_count).astype(jnp.bfloat16),
            "seq",
            scatter_dimension=1,
            tiled=True,
        ).astype(jnp.float32),
        lax.psum_scatter(
            split_rows(grad_wdown, data_count).astype(jnp.bfloat16),
            "seq",
            scatter_dimension=1,
            tiled=True,
        ).astype(jnp.float32),
    )
    owned = (
        lax.psum_scatter(parts[0], "dp", scatter_dimension=0, tiled=True),
        lax.psum_scatter(parts[1], "dp", scatter_dimension=0, tiled=True),
        lax.psum_scatter(parts[2], "dp", scatter_dimension=0, tiled=True),
        lax.psum_scatter(parts[3], "dp", scatter_dimension=0, tiled=True),
        lax.psum_scatter(parts[4], "dp", scatter_dimension=0, tiled=True),
    )
    spread = (
        lax.all_gather(owned[0].astype(jnp.bfloat16), "seq", axis=1, tiled=True).astype(
            jnp.float32
        ),
        lax.all_gather(owned[1].astype(jnp.bfloat16), "seq", axis=1, tiled=True).astype(
            jnp.float32
        ),
        lax.all_gather(owned[2].astype(jnp.bfloat16), "seq", axis=1, tiled=True).astype(
            jnp.float32
        ),
        lax.all_gather(owned[3].astype(jnp.bfloat16), "seq", axis=1, tiled=True).astype(
            jnp.float32
        ),
        lax.all_gather(owned[4].astype(jnp.bfloat16), "seq", axis=1, tiled=True).astype(
            jnp.float32
        ),
    )
    final_gain = spread[0].reshape(-1)
    final_joint = spread[1].reshape(spread[1].shape[1], -1)
    final_out = spread[2].reshape(spread[2].shape[1], -1)
    final_up = spread[3].reshape(spread[3].shape[1], -1)
    final_down = spread[4].reshape(spread[4].shape[1], -1)
    final_qkv = final_joint[:, :qkv_cols]
    final_ada = final_joint[:, qkv_cols:]
    return (
        result.astype(jnp.bfloat16),
        grad_inputs.astype(jnp.bfloat16),
        final_gain,
        final_qkv,
        final_out,
        final_ada,
        final_up,
        final_down,
    )


def solution(mesh):
    placed = (
        P(("dp", "seq"), None),
        P("dp"),
        P("dp", None),
        P("dp", None),
        P("dp", None),
        P("dp", None),
        P("dp", None),
        P(("dp", "seq"), None),
        P("dp", None),
        P("dp"),
    )
    return jax.shard_map(
        body,
        mesh=mesh,
        in_specs=placed,
        out_specs=(
            P(("dp", "seq"), None),
            P(("dp", "seq"), None),
            P("dp"),
            P("dp", None),
            P("dp", None),
            P("dp", None),
            P("dp", None),
            P("dp", None),
        ),
        check_vma=False,
    )
```

profile of v0, /device:TPU:0, one launch (start us, length us, event | category | flops | bytes accessed | tf_op | source)
XLA Modules:
  0.0 863.8 jit_solution(9710499089409813553)
XLA Ops:
  12.9 23.2 %all-reduce = bf16[768]{0:T(1024)(128)(2,1)S(1)} all-reduce(bf16[768]{0:T(1024)(128)(2,1)S(1)} %dynamic-update-slice), channel_id=1, replica_groups=mesh['dp'=8,'seq'=4] {'dp'}, use_global_device_ids=true, to_apply=%add | all-reduce | flops 768 | bytes 3072
  39.3 39.0 %all-gather.6.cloned.1.call-done = bf16[768,2304]{1,0:T(8,128)(2,1)} async-done(((bf16[96,2304]{1,0:T(8,128)(2,1)}), bf16[768,2304]{1,0:T(8,128)(2,1)}) %all-gather.6.cloned.1.call-update) | async-done | bytes 3538960 | tf_op jit(solution)/shard_map/all_gather | solution.py:96
  78.3 3.7 fusion.85
  83.8 3.5 all-to-all-start
  89.9 13.3 %all-to-all-done = bf16[256,3,4,192]{0,3,1,2:T(8,128)(2,1)S(1)} async-done(((bf16[256,3,4,192]{0,3,1,2:T(8,128)(2,1)}), bf16[256,3,4,192]{0,3,1,2:T(8,128)(2,1)S(1)}, u32[]{:S(2)}, u32[]{:S(2)}) %all-to-all-start) | async-done | bytes 1179680 | tf_op jit(solution)/shard_map/all_to_all | solution.py:122
  106.9 25.5 %while.30 = (s32[]{:T(128)}, bf16[2,512,3,64]{1,3,2,0:T(8,128)(2,1)S(1)}, f32[2,3,512]{2,1,0:T(4,128)}, s32[]{:T(128)}, s32[2]{0:T(128)S(1)}, /*index=5*/s32[]{:...) while((s32[]{:T(128)}, ...), condition=%wide.region_5.6_spmd.clone.clone, body=%wide.region_2.5_spmd.clone.clone.sunk | while | flops 422682112 | bytes 22220956 | solution.py:156
  108.8 1.9 convert_add_fusion.10
  111.7 2.3 fusion.141
  115.8 3.2 fusion.143
  121.5 1.9 convert_add_fusion.10
  124.5 2.3 fusion.141
  128.6 3.2 fusion.143
  133.8 3.5 all-to-all-start.1
  137.8 6.4 all-gather.10.cloned.1.call-done
  144.2 2.6 convolution_reduce_fusion
  146.8 39.1 %all-gather.8.cloned.1.call-done = bf16[768,768]{1,0:T(8,128)(2,1)} async-done(((bf16[96,768]{1,0:T(8,128)(2,1)}), bf16[768,768]{1,0:T(8,128)(2,1)}) %all-gather.8.cloned.1.call-update) | async-done | bytes 1179664 | tf_op jit(solution)/shard_map/all_gather | solution.py:97
  186.0 1.9 fusion.94
  188.1 78.6 %all-gather.12.cloned.1.call-done = bf16[768,3072]{1,0:T(8,128)(2,1)} async-done(((bf16[96,3072]{1,0:T(8,128)(2,1)}), bf16[768,3072]{1,0:T(8,128)(2,1)}) %all-gather.12.cloned.1.call-update) | async-done | bytes 4718608 | tf_op jit(solution)/shard_map/all_gather | solution.py:101
  266.7 5.5 fusion.87
  272.2 74.6 %all-gather.14.cloned.1.call-done = bf16[3072,768]{1,0:T(8,128)(2,1)} async-done(((bf16[384,768]{1,0:T(8,128)(2,1)}), bf16[3072,768]{1,0:T(8,128)(2,1)}) %all-gather.14.cloned.1.call-update) | async-done | bytes 4718608 | tf_op jit(solution)/shard_map/all_gather | solution.py:102
  346.8 6.7 fusion.56
  353.6 2.2 multiply_reduce_fusion.1
  357.4 3.5 fusion.72
  362.6 6.4 convolution_convert_fusion
  371.7 3.5 all-to-all-start.2
  375.4 3.0 convolution_convert_fusion.1
  378.4 2.6 copy.99
  381.0 5.4 all-to-all-done.2
  387.8 45.0 %while.31 = (s32[]{:T(128)}, f32[1024,3,64]{0,2,1:T(8,128)}, f32[1024,3,64]{0,2,1:T(8,128)}, bf16[2,512,3,64]{1,3,2,0:T(8,128)(2,1)}, bf16[2,512,3,64]{1,3,2,0:T...) while((s32[]{:T(128)}, f32[1024,3,64]{0,2,1:T(8,128)}, ...), condition=%wide.region_12.13_spmd.clone.clone, body=%wide.region_10.12_spmd.clone.clone.sunk | while | flops 1032363520 | bytes 110420320 | solution.py:226
  387.8 1.9 fusion.153
  392.3 1.8 convert_add_fusion.12
  395.2 3.8 multiply_reduce_fusion.7
  399.0 1.8 multiply_convert_fusion.6
  400.9 2.7 fusion.154
  404.2 4.0 fusion.155
  410.0 1.9 fusion.153
  417.5 3.8 multiply_reduce_fusion.7
  421.3 1.8 multiply_convert_fusion.6
  423.1 2.9 fusion.154
  426.6 4.3 fusion.155
  437.0 2.5 copy.80
  439.5 3.6 all-to-all-start.3
  443.4 2.2 multiply_convert_fusion.1
  445.6 30.9 %all-to-all-done.3 = bf16[1024,3,1,192]{3,1,2,0:T(4,128)(2,1)S(1)} async-done(((bf16[1024,3,1,192]{3,1,2,0:T(4,128)(2,1)}), bf16[1024,3,1,192]{3,1,2,0:T(4,128)(2,1)S(1)}, u32[]{:S(2)}, u32[]{:S(2)}) %all-to-all-start.3) | async-done | bytes 1179680 | tf_op jit(solution)/shard_map/all_to_all | solution.py:234
  476.5 2.8 copy.84
  482.6 5.5 pad_maximum_fusion
  488.0 6.7 copy.95
  497.6 1.9 copy.100
  499.5 2.1 copy_convert_fusion.1
  501.7 56.8 %reduce-scatter.27.cloned.1.call-done = bf16[24,36864]{1,0:T(8,128)(2,1)} async-done(((bf16[96,36864]{1,0:T(8,128)(2,1)}), bf16[24,36864]{1,0:T(8,128)(2,1)}) %reduce-scatter.27.cloned.1.call-update) | async-done | bytes 1769488
  558.5 2.0 copy.96
  560.5 2.5 copy_convert_fusion
  564.3 3.5 fusion.69
  567.8 5.7 all-reduce.2
  573.6 21.7 %all-reduce.3 = bf16[8,24,1]{1,0,2:T(8,128)(2,1)S(1)} all-reduce(f32[8,24,1]{1,0,2:T(8,128)S(1)} %dynamic-slice_convert_fusion), channel_id=3, replica_groups=mesh['dp'=8,'seq'=4] {'dp'}, use_global_device_ids=true, to_apply=%region_17.18.clone | all-reduce | flops 192 | bytes 1152
  596.2 5.6 all-reduce.1
  603.4 21.1 %reduce-scatter.19.cloned.1.call-done = f32[1,24,768]{2,1,0:T(8,128)} async-done(((f32[8,24,768]{2,1,0:T(8,128)}), f32[1,24,768]{2,1,0:T(8,128)}) %reduce-scatter.19.cloned.1.call-update) | async-done | bytes 73744 | tf_op jit(solution)/shard_map/reduce_scatter | solution.py:290
  625.3 5.5 all_gather.41
  631.5 59.9 %reduce-scatter.25.cloned.1.call-done = bf16[1,96,768]{2,1,0:T(8,128)(2,1)} async-done(((bf16[8,96,768]{2,1,0:T(8,128)(2,1)}), bf16[1,96,768]{2,1,0:T(8,128)(2,1)}) %reduce-scatter.25.cloned.1.call-update) | async-done | bytes 147472 | tf_op jit(solution)/shard_map/reduce_scatter | solution.py:292
  691.4 7.7 all_gather.43
  700.2 63.0 %reduce-scatter.21.cloned.1.call-done = f32[1,24,3072]{2,1,0:T(8,128)} async-done(((f32[8,24,3072]{2,1,0:T(8,128)}), f32[1,24,3072]{2,1,0:T(8,128)}) %reduce-scatter.21.cloned.1.call-update) | async-done | bytes 294928 | tf_op jit(solution)/shard_map/reduce_scatter | solution.py:291
  764.2 7.5 all_gather.42
  772.8 72.6 %reduce-scatter.17.cloned.1.call-done = f32[1,24,4608]{2,1,0:T(8,128)} async-done(((f32[8,24,4608]{2,1,0:T(8,128)}), f32[1,24,4608]{2,1,0:T(8,128)}) %reduce-scatter.17.cloned.1.call-update) | async-done | bytes 442384 | tf_op jit(solution)/shard_map/reduce_scatter | solution.py:289
  846.5 9.1 %all_gather.40 = bf16[1,96,4608]{2,1,0:T(8,128)(2,1)S(1)} all-gather(bf16[1,24,4608]{2,1,0:T(8,128)(2,1)S(1)} %convert_element_type.256), channel_id=1, replica_groups=mesh['dp'=8,'seq'=4] {'seq'}, dimensions={1}, use_global_device_ids=true | all-gather | bytes 1105920 | tf_op jit(solution)/shard_map/all_gather | solution.py:298
  (210 shorter events, 70.1 us)
Async XLA Ops:
  7.2 71.1 %all-gather.6.cloned.1.call-start = ((), (), s32[]{:S(2)}) async-start(), calls=%async_computation.12 | async-start | bytes 3981312 | tf_op jit(solution)/shard_map/all_gather | solution.py:96
  7.9 136.3 %all-gather.10.cloned.1.call-start = ((), (), s32[]{:S(2)}) async-start(), calls=%async_computation.14 | async-start | bytes 3981312 | tf_op jit(solution)/shard_map/all_gather | solution.py:100
  8.6 177.3 %all-gather.8.cloned.1.call-start = ((), (), s32[]{:S(2)}) async-start(), calls=%async_computation.13 | async-start | bytes 1327104 | tf_op jit(solution)/shard_map/all_gather | solution.py:97
  9.4 257.3 %all-gather.12.cloned.1.call-start = ((), (), s32[]{:S(2)}) async-start(), calls=%async_computation.15 | async-start | bytes 5308416 | tf_op jit(solution)/shard_map/all_gather | solution.py:101
  36.1 46.0 %copy-start.13 = (f32[768]{0:T(1024)}, f32[768]{0:T(1024)S(1)}, u32[]{:S(2)}) copy-start(f32[768]{0:T(1024)S(1)} %convert_element_type.231) | copy-start | bytes 9220
  37.2 44.8 %copy-start.16 = (f32[256]{0:T(256)}, f32[256]{0:T(256)S(1)}, u32[]{:S(2)}) copy-start(f32[256]{0:T(256)S(1)} %broadcast_multiply_fusion.6) | copy-start | bytes 3076
  38.5 43.6 %copy-start.18 = (f32[256]{0:T(256)}, f32[256]{0:T(256)S(1)}, u32[]{:S(2)}) copy-start(f32[256]{0:T(256)S(1)} %add_rsqrt_fusion.1) | copy-start | bytes 3076
  39.3 42.9 %copy-start.11 = (f32[256,32]{0,1:T(8,128)}, f32[256,32]{0,1:T(8,128)S(1)}, u32[]{:S(2)}) copy-start(f32[256,32]{0,1:T(8,128)S(1)} %get-tuple-element.453) | copy-start | bytes 98308
  82.7 6.6 copy-start.24
  83.8 19.4 %all-to-all-start = ((bf16[256,3,4,192]{0,3,1,2:T(8,128)(2,1)}), bf16[256,3,4,192]{0,3,1,2:T(8,128)(2,1)S(1)}, u32[]{:S(2)}, u32[]{:S(2)}) async-start(bf16[256,3,4,192]{0,3,1,2:T(8,128)(2,1)} %copy.70), calls=%async_computation | async-start | bytes 2359296 | tf_op jit(solution)/shard_map/all_to_all | solution.py:122
  87.4 259.4 %all-gather.14.cloned.1.call-start = ((), (), s32[]{:S(2)}) async-start(), calls=%async_computation.16 | async-start | bytes 5308416 | tf_op jit(solution)/shard_map/all_gather | solution.py:102
  132.4 14.4 %copy-start.28 = (s32[2]{0:T(128)}, s32[2]{0:T(128)S(1)}, u32[]{:S(2)}) copy-start(s32[2]{0:T(128)S(1)} %get-tuple-element.735) | copy-start | bytes 28
  132.8 53.2 %copy-start.3 = (bf16[256,768]{1,0:T(8,128)(2,1)S(1)}, bf16[256,768]{1,0:T(8,128)(2,1)}, u32[]{:S(2)}) copy-start(bf16[256,768]{1,0:T(8,128)(2,1)} %param.14) | copy-start | bytes 1179652
  133.8 52.2 %all-to-all-start.1 = ((bf16[4,256,192]{1,2,0:T(8,128)(2,1)}), bf16[4,256,192]{1,2,0:T(8,128)(2,1)S(1)}, u32[]{:S(2)}, u32[]{:S(2)}) async-start(bf16[4,256,192]{1,2,0:T(8,128)(2,1)} %copy.74), calls=%async_computation.1 | async-start | bytes 786432 | tf_op jit(solution)/shard_map/all_to_all | solution.py:157
  137.2 357.6 %reduce-scatter.29.cloned.1.call-start = ((), (), s32[]{:S(2)}) async-start(), calls=%async_computation.23 | async-start | bytes 1474560
  266.7 80.1 %copy-start.27 = (bf16[256,768]{1,0:T(8,128)(2,1)S(1)}, bf16[256,768]{1,0:T(8,128)(2,1)}, u32[]{:S(2)}) copy-start(bf16[256,768]{1,0:T(8,128)(2,1)} %param.21) | copy-start | bytes 1179652
  346.8 6.8 copy-start.25
  353.5 2.2 copy-start.8
  353.6 2.9 copy-start.26
  353.6 3.9 copy-start.30
  360.9 8.1 copy-start.5
  362.5 134.3 %reduce-scatter.23.cloned.1.call-start = ((), (), s32[]{:S(2)}) async-start(), calls=%async_computation.20 | async-start | bytes 5898240 | tf_op jit(solution)/shard_map/reduce_scatter | solution.py:280
  368.9 1.3 copy-start.7
  371.7 14.7 %all-to-all-start.2 = ((bf16[256,4,192]{0,2,1:T(8,128)(2,1)}), bf16[256,4,192]{0,2,1:T(8,128)(2,1)S(1)}, u32[]{:S(2)}, u32[]{:S(2)}) async-start(bf16[256,4,192]{0,2,1:T(8,128)(2,1)} %bitcast.16), calls=%async_computation.2 | async-start | bytes 786432 | tf_op jit(solution)/shard_map/all_to_all | solution.py:192
  375.1 122.4 %reduce-scatter.31.cloned.1.call-start = ((), (), s32[]{:S(2)}) async-start(), calls=%async_computation.24 | async-start | bytes 5898240
  381.0 6.8 copy-start.29
  389.7 9.3 %copy-start = (f32[3,512,1024]{2,1,0:T(8,128)}, f32[3,512,1024]{2,1,0:T(8,128)S(1)}, u32[]{:S(2)}) copy-start(f32[3,512,1024]{2,1,0:T(8,128)S(1)} %fusion.153) | copy-start | bytes 18874372 | tf_op jit(solution)/shard_map/while
  395.2 3.8 copy-start.2
  400.8 3.3 copy-start.1
  404.2 4.0 copy-start.9
  409.3 0.8 copy-start.10
  412.0 9.3 %copy-start = (f32[3,512,1024]{2,1,0:T(8,128)}, f32[3,512,1024]{2,1,0:T(8,128)S(1)}, u32[]{:S(2)}) copy-start(f32[3,512,1024]{2,1,0:T(8,128)S(1)} %fusion.153) | copy-start | bytes 18874372 | tf_op jit(solution)/shard_map/while
  417.5 3.8 copy-start.2
  423.1 3.5 copy-start.1
  426.6 4.3 copy-start.9
  432.0 0.8 copy-start.10
  436.9 6.4 copy-start.21
  436.9 6.4 copy-start.22
  436.9 6.4 copy-start.23
  436.9 6.5 copy-start.20
  439.5 37.0 %all-to-all-start.3 = ((bf16[1024,3,1,192]{3,1,2,0:T(4,128)(2,1)}), bf16[1024,3,1,192]{3,1,2,0:T(4,128)(2,1)S(1)}, u32[]{:S(2)}, u32[]{:S(2)}) async-start(bf16[1024,3,1,192]{3,1,2,0:T(4,128)(2,1)} %copy.80), calls=%async_computation.3 | async-start | bytes 4194304 | tf_op jit(solution)/shard_map/all_to_all | solution.py:234
  443.1 115.4 %reduce-scatter.27.cloned.1.call-start = ((), (), s32[]{:S(2)}) async-start(), calls=%async_computation.22 | async-start | bytes 8847360
  479.5 0.8 copy-start.12
  479.5 0.8 copy-start.15
  480.3 1.0 copy-start.4
  480.3 1.0 copy-start.14
  480.3 1.0 copy-start.17
  480.3 1.0 copy-start.19
  494.8 129.7 %reduce-scatter.19.cloned.1.call-start = ((), (), s32[]{:S(2)}) async-start(), calls=%async_computation.18 | async-start | bytes 663552 | tf_op jit(solution)/shard_map/reduce_scatter | solution.py:290
  496.8 194.6 %reduce-scatter.25.cloned.1.call-start = ((), (), s32[]{:S(2)}) async-start(), calls=%async_computation.21 | async-start | bytes 1327104 | tf_op jit(solution)/shard_map/reduce_scatter | solution.py:292
  497.5 265.7 %reduce-scatter.21.cloned.1.call-start = ((), (), s32[]{:S(2)}) async-start(), calls=%async_computation.19 | async-start | bytes 2654208 | tf_op jit(solution)/shard_map/reduce_scatter | solution.py:291
  501.7 343.8 %reduce-scatter.17.cloned.1.call-start = ((), (), s32[]{:S(2)}) async-start(), calls=%async_computation.17 | async-start | bytes 3981312 | tf_op jit(solution)/shard_map/reduce_scatter | solution.py:289
  564.2 38.1 %copy-start.6 = (f32[256,768]{1,0:T(8,128)S(1)}, f32[256,768]{1,0:T(8,128)}, u32[]{:S(2)}) copy-start(f32[256,768]{1,0:T(8,128)} %copy-done.5) | copy-start | bytes 2359300
Sparse Core Ops, SparseCore 0:
  10.2 68.0 all-gather.5
  80.5 63.6 all-gather.9
  146.4 39.5 all-gather.7
  188.0 78.6 all-gather.11
  268.7 78.0 all-gather.13
  362.6 27.1 reduce-scatter.28
  392.6 45.1 reduce-scatter.22
  440.3 55.2 reduce-scatter.30
  498.2 60.2 reduce-scatter.26
  562.2 62.1 reduce-scatter.18
  628.2 63.1 reduce-scatter.24
  695.2 67.9 reduce-scatter.20
  767.3 78.1 reduce-scatter.16
where the time goes:
time: 873 us; the launch traced here: 864 us
  waiting for transfers between devices  565 us (65%)
  blocking collectives  86 us (10%)
  matrix products  79.7 us (9%)
  other arithmetic  53.6 us (6%)
  local copies, waits for them, and re-layouts  46.8 us (5%)
  between operations  17.3 us (2%)
  starting transfers between devices  15.4 us (2%)
    all_gather x1, waiting for transfers between devices, body(): lax.all_gather(w_up, 'dp', axis=0, tiled=True)  78.6 us
    all_gather x1, waiting for transfers between devices, body(): lax.all_gather(w_down, 'dp', axis=0, tiled=True)  74.6 us
    reduce_scatter x1, waiting for transfers between devices, body(): lax.psum_scatter(parts[1], 'dp', scatter_dimension=0, tiled=True)  72.6 us
    reduce_scatter x1, waiting for transfers between devices, body(): lax.psum_scatter(parts[3], 'dp', scatter_dimension=0, tiled=True)  63 us
    unnamed x16, waiting for transfers between devices  60.7 us
    reduce_scatter x1, waiting for transfers between devices, body(): lax.psum_scatter(parts[4], 'dp', scatter_dimension=0, tiled=True)  59.9 us
    unnamed x4, blocking collectives  56.3 us
    all_gather x1, waiting for transfers between devices, body(): lax.all_gather(w_out, 'dp', axis=0, tiled=True)  39.1 us
  transfers between devices with their start and end apart: 17, of which 13 were waited for; matrix products, arithmetic and copies ran while one was open for 18% of the time, Pallas kernels for 0%

commit v1 on v0

--- a/solution.py
+++ b/solution.py
@@ -8,6 +8,23 @@
 HEAD_DIM = 64
 eps = 1e-05
 neg_fill = -1e30
+
+
+def in_order(parts, dim):
+    dims = list(parts.shape[1:])
+    dims[dim] *= parts.shape[0]
+    return jnp.moveaxis(parts, 0, dim).reshape(dims)
+
+
+def gather_around(shard, axis, dim):
+    length = lax.axis_size(axis)
+    right = [(i, (i + 1) % length) for i in range(length)]
+    tiles = [shard]
+    while len(tiles) < length:
+        tiles.append(lax.ppermute(tiles[-1], axis, right))
+    mine = lax.axis_index(axis)
+    tiles = jnp.stack(tiles)[(mine - jnp.arange(length)) % length]
+    return in_order(tiles, dim)
 
 
 def layer_norm(values_in):
@@ -98,7 +115,7 @@
     )
     ada_weight, up_weight, down_weight = (
         lax.all_gather(w_ada, "dp", axis=0, tiled=True),
-        lax.all_gather(w_up, "dp", axis=0, tiled=True),
+        gather_around(w_up, "dp", 0),
         lax.all_gather(w_down, "dp", axis=0, tiled=True),
     )
     gain_float = gain_full.astype(jnp.float32)

time: 873 us -> 849 us (0.973)
  waiting for transfers between devices: 565 us -> 513 us
  local copies, waits for them, and re-layouts: 46.8 us -> 59.4 us
    ppermute x0 -> x7, waiting for transfers between devices: none -> 130 us  [gather_around(): tiles.append(lax.ppermute(tiles[-1], axis, right))]
    all_gather x1 -> x0, waiting for transfers between devices: 78.6 us -> none  [body(): lax.all_gather(w_up, 'dp', axis=0, tiled=True)]
    all_gather x1, waiting for transfers between devices: 39.1 us -> 0.02 us  [body(): lax.all_gather(w_out, 'dp', axis=0, tiled=True)]
    all_gather x1, waiting for transfers between devices: 39 us -> 0.01 us  [body(): lax.all_gather(w_qkv, 'dp', axis=0, tiled=True)]
    all_to_all x1, waiting for transfers between devices: 13.3 us -> 0.01 us  [body(): lax.all_to_all(outgoing, 'seq', split_axis=2, concat_axis=0, tiled=True)]
    all_gather x1, waiting for transfers between devices: 74.6 us -> 65.8 us  [body(): lax.all_gather(w_down, 'dp', axis=0, tiled=True)]
    unnamed x66 -> x69, local copies, waits for them, and re-layouts: 24 us -> 29.6 us
    unnamed x16 -> x15, waiting for transfers between devices: 60.7 us -> 59.8 us
  transfers between devices with their start and end apart: 17 -> 23, of which waited for: 13 -> 15; matrix products, arithmetic and copies ran while one was open for 18% -> 20% of each run, Pallas kernels for 0% -> 0%
where the time goes in v1:
time: 849 us; the launch traced here: 839 us
  waiting for transfers between devices  513 us (60%)
  blocking collectives  91.9 us (11%)
  matrix products  82.7 us (10%)
  local copies, waits for them, and re-layouts  59.4 us (7%)
  other arithmetic  52.9 us (6%)
  starting transfers between devices  20.9 us (2%)
  between operations  17.7 us (2%)
    ppermute x7, waiting for transfers between devices, gather_around(): tiles.append(lax.ppermute(tiles[-1], axis, right))  130 us
    reduce_scatter x1, waiting for transfers between devices, body(): lax.psum_scatter(parts[1], 'dp', scatter_dimension=0, tiled=True)  72.3 us
    all_gather x1, waiting for transfers between devices, body(): lax.all_gather(w_down, 'dp', axis=0, tiled=True)  65.8 us
    reduce_scatter x1, waiting for transfers between devices, body(): lax.psum_scatter(parts[3], 'dp', scatter_dimension=0, tiled=True)  63.1 us
    unnamed x4, blocking collectives  62.1 us
    reduce_scatter x1, waiting for transfers between devices, body(): lax.psum_scatter(parts[4], 'dp', scatter_dimension=0, tiled=True)  59.8 us
    unnamed x15, waiting for transfers between devices  59.8 us
    all_to_all x1, waiting for transfers between devices, body(): lax.all_to_all(stacked, 'seq', split_axis=0, concat_axis=2, tiled=True)  30.8 us
  transfers between devices with their start and end apart: 23, of which 15 were waited for; matrix products, arithmetic and copies ran while one was open for 20% of the time, Pallas kernels for 0%

profile of v1, /device:TPU:0, one launch (start us, length us, event | category | flops | bytes accessed | tf_op | source)
XLA Modules:
  0.0 838.7 jit_solution(9161201995392866725)
XLA Ops:
  9.4 3.0 collective-permute-start
  16.8 29.0 %all-reduce = bf16[768]{0:T(1024)(128)(2,1)S(1)} all-reduce(bf16[768]{0:T(1024)(128)(2,1)S(1)} %dynamic-update-slice), channel_id=1, replica_groups=mesh['dp'=8,'seq'=4] {'dp'}, use_global_device_ids=true, to_apply=%add | all-reduce | flops 768 | bytes 3072
  50.5 1.9 bitcast_dynamic-update-slice_fusion.8
  52.4 2.3 collective-permute-start.1
  55.6 26.6 %collective-permute-done.1 = bf16[96,3072]{1,0:T(8,128)(2,1)S(1)} collective-permute-done((bf16[96,3072]{1,0:T(8,128)(2,1)S(1)}, bf16[96,3072]{1,0:T(8,128)(2,1)S(1)}, u32[]{:S(2)}, u32[]{:S(2)}) %collective-permute-start.1) | collective-permute-done | bytes 589856 | tf_op jit(solution)/shard_map/ppermute | solution.py:24
  83.3 23.1 %collective-permute-done.2 = bf16[96,3072]{1,0:T(8,128)(2,1)S(1)} collective-permute-done((bf16[96,3072]{1,0:T(8,128)(2,1)S(1)}, bf16[96,3072]{1,0:T(8,128)(2,1)S(1)}, u32[]{:S(2)}, u32[]{:S(2)}) %collective-permute-start.2) | collective-permute-done | bytes 589856 | tf_op jit(solution)/shard_map/ppermute | solution.py:24
  107.2 17.0 %collective-permute-done.3 = bf16[96,3072]{1,0:T(8,128)(2,1)S(1)} collective-permute-done((bf16[96,3072]{1,0:T(8,128)(2,1)S(1)}, bf16[96,3072]{1,0:T(8,128)(2,1)S(1)}, u32[]{:S(2)}, u32[]{:S(2)}) %collective-permute-start.3) | collective-permute-done | bytes 589856 | tf_op jit(solution)/shard_map/ppermute | solution.py:24
  125.1 21.5 %collective-permute-done.4 = bf16[96,3072]{1,0:T(8,128)(2,1)S(1)} collective-permute-done((bf16[96,3072]{1,0:T(8,128)(2,1)S(1)}, bf16[96,3072]{1,0:T(8,128)(2,1)S(1)}, u32[]{:S(2)}, u32[]{:S(2)}) %collective-permute-start.4) | collective-permute-done | bytes 589856 | tf_op jit(solution)/shard_map/ppermute | solution.py:24
  147.5 28.8 %collective-permute-done.5 = bf16[96,3072]{1,0:T(8,128)(2,1)S(1)} collective-permute-done((bf16[96,3072]{1,0:T(8,128)(2,1)S(1)}, bf16[96,3072]{1,0:T(8,128)(2,1)S(1)}, u32[]{:S(2)}, u32[]{:S(2)}) %collective-permute-start.5) | collective-permute-done | bytes 589856 | tf_op jit(solution)/shard_map/ppermute | solution.py:24
  176.4 3.6 fusion.87
  181.7 3.5 all-to-all-start
  186.2 13.4 %collective-permute-done.6 = bf16[96,3072]{1,0:T(8,128)(2,1)S(1)} collective-permute-done((bf16[96,3072]{1,0:T(8,128)(2,1)S(1)}, bf16[96,3072]{1,0:T(8,128)(2,1)S(1)}, u32[]{:S(2)}, u32[]{:S(2)}) %collective-permute-start.6) | collective-permute-done | bytes 589856 | tf_op jit(solution)/shard_map/ppermute | solution.py:24
  200.5 5.3 gather_fusion
  209.5 25.0 %while.30 = (s32[]{:T(128)}, bf16[2,512,3,64]{1,3,2,0:T(8,128)(2,1)S(1)}, f32[2,3,512]{2,1,0:T(4,128)}, s32[]{:T(128)}, s32[2]{0:T(128)S(1)}, /*index=5*/s32[]{:...) while((s32[]{:T(128)}, ...), condition=%wide.region_5.6_spmd.clone.clone, body=%wide.region_2.5_spmd.clone.clone.sunk | while | flops 422682112 | bytes 22220956 | solution.py:173
  214.1 2.3 fusion.143
  218.2 3.2 fusion.145
  226.6 2.3 fusion.143
  230.7 3.2 fusion.145
  235.9 3.5 all-to-all-start.1
  239.9 2.6 convolution_reduce_fusion
  242.6 4.2 all-to-all-done.1
  246.8 1.9 fusion.96
  249.0 5.7 fusion.89
  254.6 65.8 %all-gather.11.cloned.1.call-done = bf16[3072,768]{1,0:T(8,128)(2,1)} async-done(((bf16[384,768]{1,0:T(8,128)(2,1)}), bf16[3072,768]{1,0:T(8,128)(2,1)}) %all-gather.11.cloned.1.call-update) | async-done | bytes 4718608 | tf_op jit(solution)/shard_map/all_gather | solution.py:119
  320.4 6.6 fusion.56
  327.1 5.2 multiply_reduce_fusion.1
  332.3 3.5 fusion.72
  337.5 6.4 convolution_convert_fusion
  346.6 3.5 all-to-all-start.2
  350.3 3.0 convolution_convert_fusion.1
  353.3 2.5 copy.99
  355.8 5.5 all-to-all-done.2
  362.7 44.7 %while.31 = (s32[]{:T(128)}, f32[1024,3,64]{0,2,1:T(8,128)}, f32[1024,3,64]{0,2,1:T(8,128)}, bf16[2,512,3,64]{1,3,2,0:T(8,128)(2,1)}, bf16[2,512,3,64]{1,3,2,0:T...) while((s32[]{:T(128)}, f32[1024,3,64]{0,2,1:T(8,128)}, ...), condition=%wide.region_12.13_spmd.clone.clone, body=%wide.region_10.12_spmd.clone.clone.sunk | while | flops 1032363520 | bytes 110420320 | solution.py:243
  362.7 1.9 fusion.155
  370.0 3.8 multiply_reduce_fusion.7
  375.7 2.7 fusion.156
  379.0 4.0 fusion.157
  384.9 1.9 fusion.155
  392.2 3.8 multiply_reduce_fusion.7
  397.8 2.9 fusion.156
  401.3 4.3 fusion.157
  411.6 2.5 copy.80
  414.2 3.6 all-to-all-start.3
  418.1 2.2 multiply_convert_fusion.1
  420.3 30.8 %all-to-all-done.3 = bf16[1024,3,1,192]{3,1,2,0:T(4,128)(2,1)S(1)} async-done(((bf16[1024,3,1,192]{3,1,2,0:T(4,128)(2,1)}), bf16[1024,3,1,192]{3,1,2,0:T(4,128)(2,1)S(1)}, u32[]{:S(2)}, u32[]{:S(2)}) %all-to-all-start.3) | async-done | bytes 1179680 | tf_op jit(solution)/shard_map/all_to_all | solution.py:251
  451.1 2.8 copy.84
  457.2 5.5 pad_maximum_fusion
  462.6 6.7 copy.95
  474.0 2.1 copy_convert_fusion.1
  476.2 57.1 %reduce-scatter.27.cloned.1.call-done = bf16[24,36864]{1,0:T(8,128)(2,1)} async-done(((bf16[96,36864]{1,0:T(8,128)(2,1)}), bf16[24,36864]{1,0:T(8,128)(2,1)}) %reduce-scatter.27.cloned.1.call-update) | async-done | bytes 1769488
  533.3 2.0 copy.96
  535.3 2.4 copy_convert_fusion
  539.0 3.5 fusion.69
  542.5 5.7 all-reduce.2
  548.4 21.7 %all-reduce.3 = bf16[8,24,1]{1,0,2:T(8,128)(2,1)S(1)} all-reduce(f32[8,24,1]{1,0,2:T(8,128)S(1)} %dynamic-slice_convert_fusion), channel_id=3, replica_groups=mesh['dp'=8,'seq'=4] {'dp'}, use_global_device_ids=true, to_apply=%region_17.18.clone | all-reduce | flops 192 | bytes 1152
  571.0 5.6 all-reduce.1
  578.2 21.1 %reduce-scatter.19.cloned.1.call-done = f32[1,24,768]{2,1,0:T(8,128)} async-done(((f32[8,24,768]{2,1,0:T(8,128)}), f32[1,24,768]{2,1,0:T(8,128)}) %reduce-scatter.19.cloned.1.call-update) | async-done | bytes 73744 | tf_op jit(solution)/shard_map/reduce_scatter | solution.py:307
  600.2 5.5 all_gather.37
  606.3 59.8 %reduce-scatter.25.cloned.1.call-done = bf16[1,96,768]{2,1,0:T(8,128)(2,1)} async-done(((bf16[8,96,768]{2,1,0:T(8,128)(2,1)}), bf16[1,96,768]{2,1,0:T(8,128)(2,1)}) %reduce-scatter.25.cloned.1.call-update) | async-done | bytes 147472 | tf_op jit(solution)/shard_map/reduce_scatter | solution.py:309
  666.2 7.7 all_gather.39
  675.0 63.1 %reduce-scatter.21.cloned.1.call-done = f32[1,24,3072]{2,1,0:T(8,128)} async-done(((f32[8,24,3072]{2,1,0:T(8,128)}), f32[1,24,3072]{2,1,0:T(8,128)}) %reduce-scatter.21.cloned.1.call-update) | async-done | bytes 294928 | tf_op jit(solution)/shard_map/reduce_scatter | solution.py:308
  739.1 7.5 all_gather.38
  747.7 72.3 %reduce-scatter.17.cloned.1.call-done = f32[1,24,4608]{2,1,0:T(8,128)} async-done(((f32[8,24,4608]{2,1,0:T(8,128)}), f32[1,24,4608]{2,1,0:T(8,128)}) %reduce-scatter.17.cloned.1.call-update) | async-done | bytes 442384 | tf_op jit(solution)/shard_map/reduce_scatter | solution.py:306
  821.0 9.1 %all_gather.36 = bf16[1,96,4608]{2,1,0:T(8,128)(2,1)S(1)} all-gather(bf16[1,24,4608]{2,1,0:T(8,128)(2,1)S(1)} %convert_element_type.256), channel_id=1, replica_groups=mesh['dp'=8,'seq'=4] {'seq'}, dimensions={1}, use_global_device_ids=true | all-gather | bytes 1105920 | tf_op jit(solution)/shard_map/all_gather | solution.py:315
  (228 shorter events, 85.1 us)
Async XLA Ops:
  7.2 169.2 %all-gather.5.cloned.1.call-start = ((), (), s32[]{:S(2)}) async-start(), calls=%async_computation.12 | async-start | bytes 3981312 | tf_op jit(solution)/shard_map/all_gather | solution.py:113
  7.9 232.0 %all-gather.9.cloned.1.call-start = ((), (), s32[]{:S(2)}) async-start(), calls=%async_computation.14 | async-start | bytes 3981312 | tf_op jit(solution)/shard_map/all_gather | solution.py:117
  8.6 233.9 %all-gather.7.cloned.1.call-start = ((), (), s32[]{:S(2)}) async-start(), calls=%async_computation.13 | async-start | bytes 1327104 | tf_op jit(solution)/shard_map/all_gather | solution.py:114
  9.4 311.0 %all-gather.11.cloned.1.call-start = ((), (), s32[]{:S(2)}) async-start(), calls=%async_computation.15 | async-start | bytes 5308416 | tf_op jit(solution)/shard_map/all_gather | solution.py:119
  9.4 43.0 %collective-permute-start = (bf16[96,3072]{1,0:T(8,128)(2,1)}, bf16[96,3072]{1,0:T(8,128)(2,1)S(1)}, u32[]{:S(2)}, u32[]{:S(2)}) collective-permute-start(bf16[96,3072]{1,0:T(8,128)(2,1)} %param.19), channel_id=1, source_target_pairs={{0,4},{4,8},{8,12},{12,16},{16,20},{20,24},{24,28},{28,0},{1,5},{5... | collective-permute-start | bytes 1769480 | tf_op jit(solution)/shard_map/ppermute | solution.py:24
  45.8 130.5 %copy-start.13 = (f32[768]{0:T(1024)}, f32[768]{0:T(1024)S(1)}, u32[]{:S(2)}) copy-start(f32[768]{0:T(1024)S(1)} %convert_element_type.231) | copy-start | bytes 9220
  47.0 129.4 %copy-start.16 = (f32[256]{0:T(256)}, f32[256]{0:T(256)S(1)}, u32[]{:S(2)}) copy-start(f32[256]{0:T(256)S(1)} %broadcast_multiply_fusion.6) | copy-start | bytes 3076
  48.3 128.0 %copy-start.18 = (f32[256]{0:T(256)}, f32[256]{0:T(256)S(1)}, u32[]{:S(2)}) copy-start(f32[256]{0:T(256)S(1)} %add_rsqrt_fusion.1) | copy-start | bytes 3076
  50.5 129.7 %copy-start.11 = (f32[256,32]{0,1:T(8,128)}, f32[256,32]{0,1:T(8,128)S(1)}, u32[]{:S(2)}) copy-start(f32[256,32]{0,1:T(8,128)S(1)} %get-tuple-element.453) | copy-start | bytes 98308
  52.4 123.9 %copy-start.3 = (bf16[256,768]{1,0:T(8,128)(2,1)S(1)}, bf16[256,768]{1,0:T(8,128)(2,1)}, u32[]{:S(2)}) copy-start(bf16[256,768]{1,0:T(8,128)(2,1)} %param.14) | copy-start | bytes 1179652
  52.4 29.7 %collective-permute-start.1 = (bf16[96,3072]{1,0:T(8,128)(2,1)S(1)}, bf16[96,3072]{1,0:T(8,128)(2,1)S(1)}, u32[]{:S(2)}, u32[]{:S(2)}) collective-permute-start(bf16[96,3072]{1,0:T(8,128)(2,1)S(1)} %collective-permute-done), channel_id=1, source_target_pairs={{0,4},{4,8},{8,12},{12,16},{16,20},{20,24},{24,28},{28,0},{1,5},{5... | collective-permute-start | bytes 1769480 | tf_op jit(solution)/shard_map/ppermute | solution.py:24
  82.2 24.2 %collective-permute-start.2 = (bf16[96,3072]{1,0:T(8,128)(2,1)S(1)}, bf16[96,3072]{1,0:T(8,128)(2,1)S(1)}, u32[]{:S(2)}, u32[]{:S(2)}) collective-permute-start(bf16[96,3072]{1,0:T(8,128)(2,1)S(1)} %collective-permute-done.1), channel_id=1, source_target_pairs={{0,4},{4,8},{8,12},{12,16},{16,20},{20,24},{24,28},{28,0},{1,5},{5... | collective-permute-start | bytes 1769480 | tf_op jit(solution)/shard_map/ppermute | solution.py:24
  106.4 17.8 %collective-permute-start.3 = (bf16[96,3072]{1,0:T(8,128)(2,1)S(1)}, bf16[96,3072]{1,0:T(8,128)(2,1)S(1)}, u32[]{:S(2)}, u32[]{:S(2)}) collective-permute-start(bf16[96,3072]{1,0:T(8,128)(2,1)S(1)} %collective-permute-done.2), channel_id=1, source_target_pairs={{0,4},{4,8},{8,12},{12,16},{16,20},{20,24},{24,28},{28,0},{1,5},{5... | collective-permute-start | bytes 1769480 | tf_op jit(solution)/shard_map/ppermute | solution.py:24
  124.2 22.4 %collective-permute-start.4 = (bf16[96,3072]{1,0:T(8,128)(2,1)S(1)}, bf16[96,3072]{1,0:T(8,128)(2,1)S(1)}, u32[]{:S(2)}, u32[]{:S(2)}) collective-permute-start(bf16[96,3072]{1,0:T(8,128)(2,1)S(1)} %collective-permute-done.3), channel_id=1, source_target_pairs={{0,4},{4,8},{8,12},{12,16},{16,20},{20,24},{24,28},{28,0},{1,5},{5... | collective-permute-start | bytes 1769480 | tf_op jit(solution)/shard_map/ppermute | solution.py:24
  146.6 29.7 %collective-permute-start.5 = (bf16[96,3072]{1,0:T(8,128)(2,1)S(1)}, bf16[96,3072]{1,0:T(8,128)(2,1)S(1)}, u32[]{:S(2)}, u32[]{:S(2)}) collective-permute-start(bf16[96,3072]{1,0:T(8,128)(2,1)S(1)} %collective-permute-done.4), channel_id=1, source_target_pairs={{0,4},{4,8},{8,12},{12,16},{16,20},{20,24},{24,28},{28,0},{1,5},{5... | collective-permute-start | bytes 1769480 | tf_op jit(solution)/shard_map/ppermute | solution.py:24
  176.3 23.3 %collective-permute-start.6 = (bf16[96,3072]{1,0:T(8,128)(2,1)S(1)}, bf16[96,3072]{1,0:T(8,128)(2,1)S(1)}, u32[]{:S(2)}, u32[]{:S(2)}) collective-permute-start(bf16[96,3072]{1,0:T(8,128)(2,1)S(1)} %collective-permute-done.5), channel_id=1, source_target_pairs={{0,4},{4,8},{8,12},{12,16},{16,20},{20,24},{24,28},{28,0},{1,5},{5... | collective-permute-start | bytes 1769480 | tf_op jit(solution)/shard_map/ppermute | solution.py:24
  181.7 24.1 %all-to-all-start = ((bf16[256,3,4,192]{0,3,1,2:T(8,128)(2,1)}), bf16[256,3,4,192]{0,3,1,2:T(8,128)(2,1)S(1)}, u32[]{:S(2)}, u32[]{:S(2)}) async-start(bf16[256,3,4,192]{0,3,1,2:T(8,128)(2,1)} %copy.70), calls=%async_computation | async-start | bytes 2359296 | tf_op jit(solution)/shard_map/all_to_all | solution.py:139
  234.6 5.4 copy-start.26
  235.9 10.9 %all-to-all-start.1 = ((bf16[4,256,192]{1,2,0:T(8,128)(2,1)}), bf16[4,256,192]{1,2,0:T(8,128)(2,1)S(1)}, u32[]{:S(2)}, u32[]{:S(2)}) async-start(bf16[4,256,192]{1,2,0:T(8,128)(2,1)} %copy.74), calls=%async_computation.1 | async-start | bytes 786432 | tf_op jit(solution)/shard_map/all_to_all | solution.py:174
  239.4 230.1 %reduce-scatter.29.cloned.1.call-start = ((), (), s32[]{:S(2)}) async-start(), calls=%async_computation.22 | async-start | bytes 1474560
  249.0 71.4 %copy-start.25 = (bf16[256,768]{1,0:T(8,128)(2,1)S(1)}, bf16[256,768]{1,0:T(8,128)(2,1)}, u32[]{:S(2)}) copy-start(bf16[256,768]{1,0:T(8,128)(2,1)} %param.21) | copy-start | bytes 1179652
  327.0 5.2 copy-start.8
  327.0 5.2 copy-start.24
  327.0 5.3 copy-start.28
  335.8 8.1 copy-start.5
  337.4 134.0 %reduce-scatter.23.cloned.1.call-start = ((), (), s32[]{:S(2)}) async-start(), calls=%async_computation.19 | async-start | bytes 5898240 | tf_op jit(solution)/shard_map/reduce_scatter | solution.py:297
  343.9 1.3 copy-start.7
  346.6 14.8 %all-to-all-start.2 = ((bf16[256,4,192]{0,2,1:T(8,128)(2,1)}), bf16[256,4,192]{0,2,1:T(8,128)(2,1)S(1)}, u32[]{:S(2)}, u32[]{:S(2)}) async-start(bf16[256,4,192]{0,2,1:T(8,128)(2,1)} %bitcast.26), calls=%async_computation.2 | async-start | bytes 786432 | tf_op jit(solution)/shard_map/all_to_all | solution.py:209
  350.1 122.0 %reduce-scatter.31.cloned.1.call-start = ((), (), s32[]{:S(2)}) async-start(), calls=%async_computation.23 | async-start | bytes 5898240
  355.8 6.9 copy-start.27
  364.7 9.1 %copy-start = (f32[3,512,1024]{2,1,0:T(8,128)}, f32[3,512,1024]{2,1,0:T(8,128)S(1)}, u32[]{:S(2)}) copy-start(f32[3,512,1024]{2,1,0:T(8,128)S(1)} %fusion.155) | copy-start | bytes 18874372 | tf_op jit(solution)/shard_map/while
  370.0 3.8 copy-start.2
  375.7 3.3 copy-start.1
  379.0 4.0 copy-start.9
  384.1 0.8 copy-start.10
  386.8 9.1 %copy-start = (f32[3,512,1024]{2,1,0:T(8,128)}, f32[3,512,1024]{2,1,0:T(8,128)S(1)}, u32[]{:S(2)}) copy-start(f32[3,512,1024]{2,1,0:T(8,128)S(1)} %fusion.155) | copy-start | bytes 18874372 | tf_op jit(solution)/shard_map/while
  392.2 3.8 copy-start.2
  397.8 3.5 copy-start.1
  401.3 4.3 copy-start.9
  406.6 0.8 copy-start.10
  411.6 6.4 copy-start.21
  411.6 6.4 copy-start.22
  411.6 6.4 copy-start.23
  411.6 6.5 copy-start.20
  414.2 36.9 %all-to-all-start.3 = ((bf16[1024,3,1,192]{3,1,2,0:T(4,128)(2,1)}), bf16[1024,3,1,192]{3,1,2,0:T(4,128)(2,1)S(1)}, u32[]{:S(2)}, u32[]{:S(2)}) async-start(bf16[1024,3,1,192]{3,1,2,0:T(4,128)(2,1)} %copy.80), calls=%async_computation.3 | async-start | bytes 4194304 | tf_op jit(solution)/shard_map/all_to_all | solution.py:251
  417.8 115.5 %reduce-scatter.27.cloned.1.call-start = ((), (), s32[]{:S(2)}) async-start(), calls=%async_computation.21 | async-start | bytes 8847360
  454.1 0.8 copy-start.12
  454.1 0.8 copy-start.15
  454.8 1.0 copy-start.4
  454.8 1.0 copy-start.14
  454.9 1.0 copy-start.17
  454.9 1.0 copy-start.19
  469.4 129.9 %reduce-scatter.19.cloned.1.call-start = ((), (), s32[]{:S(2)}) async-start(), calls=%async_computation.17 | async-start | bytes 663552 | tf_op jit(solution)/shard_map/reduce_scatter | solution.py:307
  471.4 194.8 %reduce-scatter.25.cloned.1.call-start = ((), (), s32[]{:S(2)}) async-start(), calls=%async_computation.20 | async-start | bytes 1327104 | tf_op jit(solution)/shard_map/reduce_scatter | solution.py:309
  472.0 266.1 %reduce-scatter.21.cloned.1.call-start = ((), (), s32[]{:S(2)}) async-start(), calls=%async_computation.18 | async-start | bytes 2654208 | tf_op jit(solution)/shard_map/reduce_scatter | solution.py:308
  476.1 343.8 %reduce-scatter.17.cloned.1.call-start = ((), (), s32[]{:S(2)}) async-start(), calls=%async_computation.16 | async-start | bytes 3981312 | tf_op jit(solution)/shard_map/reduce_scatter | solution.py:306
  539.0 38.1 %copy-start.6 = (f32[256,768]{1,0:T(8,128)S(1)}, f32[256,768]{1,0:T(8,128)}, u32[]{:S(2)}) copy-start(f32[256,768]{1,0:T(8,128)} %copy-done.5) | copy-start | bytes 2359300
Sparse Core Ops, SparseCore 0:
  10.2 84.6 all-gather.4
  97.0 97.7 all-gather.8
  197.0 42.6 all-gather.6
  241.7 78.6 all-gather.10
  337.5 27.2 reduce-scatter.28
  367.3 45.1 reduce-scatter.22
  415.0 55.1 reduce-scatter.30
  472.9 60.3 reduce-scatter.26
  537.1 62.0 reduce-scatter.18
  602.9 63.2 reduce-scatter.24
  670.1 67.9 reduce-scatter.20
  742.0 77.9 reduce-scatter.16
